TPU v7x, 256 devices: a whole 4x4x8 slice. The times are simulated.
256 devices in a mesh: seg: 64 (over y, z, core), ch: 4 (over x).
Axes of the slice: x: 4, y: 4, z: 8, core: 2. Of those that a mesh axis runs over, the one named last changes fastest.
Arguments:
- voxels: bfloat16 [65536, 256], P('seg'), may hold values from -6 to 6
- neighbours: int32 [27, 65536], P(None, 'seg'), may hold values from -1 to 65535, as said below
- send_perm: int32 [64, 1024], P('seg'), may hold values from 0 to 1023, each once within a row
- send_counts: int32 [64, 64], replicated, may hold values from 0 to 32, as said below
- conv_weight: bfloat16 [27, 256, 256], P(None, None, 'ch'), may hold values from -0.078125 to 0.078125
- qkv_first: bfloat16 [256, 3, 256], P(None, None, 'ch'), may hold values from -3 to 3
- out_first: bfloat16 [256, 256], replicated, may hold values from -0.375 to 0.375
- qkv_second: bfloat16 [256, 3, 256], P(None, None, 'ch'), may hold values from -3 to 3
- out_second: bfloat16 [256, 256], replicated, may hold values from -0.375 to 0.375
Outputs:
- encoded: bfloat16 [65536, 256], P('seg', 'ch')
Inputs may be any that keep to these rules, and one draw needn't show every extreme that they name: `neighbours`: -1 marks an absent neighbour; any other entry is a voxel within 128 positions of the entry's own voxel along the z-order curve, and the middle offset is the voxel itself. `send_counts`: each row sums to 1024; some Hilbert segment receives exactly 32 voxels from every z-order segment.
All inputs are finite; a program needn't handle non-finite values.
Results may differ from a plain program's by a relative error of at most 0.02.
Values may be sent and summed in bfloat16 or wider, within the bound.
No kernel may reach another device: no remote copies, remote signals or barrier semaphores. Data moves between devices by JAX's collectives and lax.ppermute only.
A program may use at most 64 MiB of HBM per device.

v0:
```python
import jax
import jax.numpy as jnp
from jax import lax
from jax.sharding import PartitionSpec as P

HD = 16
PATCH = 1024
KOFF = 27
HALO = 128
NORM_EPS = 1e-05
MASKED_SCORE = -1e30


def extended(cells, sides, width):
    for axis, dim in sides:
        count = lax.axis_size(axis)
        ends = count - 1
        head = lax.slice_in_dim(cells, 0, width, axis=dim)
        tail = lax.slice_in_dim(cells, cells.shape[dim] - width, cells.shape[dim], axis=dim)
        cells = jnp.concatenate(
            [
                lax.ppermute(tail, axis, [(i, (i + 1) % count) for i in range(ends)]),
                cells,
                lax.ppermute(head, axis, [((i + 1) % count, i) for i in range(ends)]),
            ],
            axis=dim,
        )
    return cells


def layer_norm(rows_in):
    values32 = rows_in.astype(jnp.float32)
    centre = values32 - jnp.mean(values32, axis=-1, keepdims=True)
    spread = jnp.mean(centre * centre, axis=-1, keepdims=True)
    return (centre * lax.rsqrt(spread + NORM_EPS)).astype(jnp.bfloat16)


def project(normed, weight):
    width_in, stacked, local_cols = weight.shape
    product = jnp.dot(
        normed, weight.reshape(width_in, stacked * local_cols), preferred_element_type=jnp.float32
    )
    return product.astype(jnp.bfloat16).reshape(normed.shape[0], stacked, local_cols // HD, HD)


def patch_attention(qkv_rows, key_live):
    count_rows, stacked, head_count, head_dim = qkv_rows.shape
    query_rows = min(512, PATCH)
    score_scale = head_dim ** (-0.5)
    grouped = qkv_rows.reshape(count_rows // PATCH, PATCH, stacked, head_count, head_dim)
    masks = key_live.reshape(count_rows // PATCH, PATCH)

    def one_patch(packed_item):
        patch_rows, live_keys = packed_item
        key_rows = patch_rows[:, 1]
        value_rows = patch_rows[:, 2]
        query_blocks = patch_rows[:, 0].reshape(
            PATCH // query_rows, query_rows, head_count, head_dim
        )

        def one_block(query_block):
            scores = (
                jnp.einsum(
                    "qhd,khd->hqk", query_block, key_rows, preferred_element_type=jnp.float32
                )
                * score_scale
            )
            scores = jnp.where(live_keys[None, None, :], scores, MASKED_SCORE)
            peak = jnp.max(scores, axis=2, keepdims=True)
            powered = jnp.exp(scores - peak)
            normaliser = jnp.sum(powered, axis=2)
            blended = jnp.einsum(
                "hqk,khd->qhd",
                powered.astype(jnp.bfloat16),
                value_rows,
                preferred_element_type=jnp.float32,
            )
            return (blended / jnp.transpose(normaliser)[:, :, None]).astype(jnp.bfloat16)

        return lax.map(one_block, query_blocks).reshape(PATCH, head_count * head_dim)

    return lax.map(one_patch, (grouped, masks)).reshape(count_rows, head_count * head_dim)


def local(
    voxels,
    neighbours,
    send_perm,
    send_counts,
    conv_weight,
    qkv_first,
    out_first,
    qkv_second,
    out_second,
):
    seg_index = lax.axis_index("seg")
    seg_count = lax.axis_size("seg")
    ch_index = lax.axis_index("ch")
    rows_dev, channels = voxels.shape
    quarter = conv_weight.shape[2]
    bucket_rows = 2 * rows_dev // seg_count
    total_slots = seg_count * bucket_rows
    padded = extended(voxels, (("seg", 0),), HALO)
    first_row = seg_index * rows_dev - HALO
    padded_rows = rows_dev + 2 * HALO

    def conv_step(kernel_index, running):
        target = neighbours[kernel_index]
        local_row = jnp.clip(target - first_row, 0, padded_rows - 1)
        picked = jnp.take(padded, local_row, axis=0)
        picked = jnp.where((target >= 0)[:, None], picked, jnp.zeros((), jnp.bfloat16))
        return running + jnp.dot(
            picked, conv_weight[kernel_index], preferred_element_type=jnp.float32
        )

    conv_sum = lax.fori_loop(0, KOFF, conv_step, jnp.zeros((rows_dev, quarter), jnp.float32))
    own_cols = lax.dynamic_slice_in_dim(voxels, ch_index * quarter, quarter, 1)
    mixed_a_part = (own_cols.astype(jnp.float32) + conv_sum).astype(jnp.bfloat16)
    mixed_a = lax.all_gather(mixed_a_part, "ch", axis=1, tiled=True)
    qkv_a = project(layer_norm(mixed_a), qkv_first)
    heads_a = patch_attention(qkv_a, jnp.ones((rows_dev,), bool))
    out_rows = lax.dynamic_slice_in_dim(out_first, ch_index * quarter, quarter, 0)
    partial_one = jnp.dot(heads_a, out_rows, preferred_element_type=jnp.float32)
    attn_one = lax.psum(partial_one.astype(jnp.bfloat16), "ch").astype(jnp.float32)
    mixed_b = (mixed_a.astype(jnp.float32) + attn_one).astype(jnp.bfloat16)
    mixed_b_part = lax.dynamic_slice_in_dim(mixed_b, ch_index * quarter, quarter, 1)
    counts_row = lax.dynamic_index_in_dim(send_counts, seg_index, 0, keepdims=False)
    send_off = jnp.cumsum(counts_row) - counts_row
    send_end = send_off + counts_row
    send_order = send_perm[0]
    bucket_pos = send_off[:, None] + jnp.arange(bucket_rows, dtype=jnp.int32)[None, :]
    send_rows = send_order[jnp.clip(bucket_pos, 0, rows_dev - 1)].reshape(-1)
    counts_col = lax.dynamic_index_in_dim(send_counts, seg_index, 1, keepdims=False)
    recv_off = jnp.cumsum(counts_col) - counts_col
    recv_end = recv_off + counts_col
    slots = jnp.arange(total_slots, dtype=jnp.int32)
    source = jnp.minimum(
        jnp.sum((recv_end[None, :] <= slots[:, None]).astype(jnp.int32), axis=1), seg_count - 1
    )
    within = jnp.clip(slots - recv_off[source], 0, bucket_rows - 1)
    flat_from = source * bucket_rows + within
    live_keys = slots < jnp.sum(counts_col)
    qkv_b = project(layer_norm(mixed_b), qkv_second)
    head_local = qkv_b.shape[2]
    outgoing = jnp.take(qkv_b.reshape(rows_dev, 3 * quarter), send_rows, axis=0).reshape(
        seg_count, bucket_rows, 3 * quarter
    )
    arrived = lax.all_to_all(outgoing, "seg", split_axis=0, concat_axis=0, tiled=True).reshape(
        total_slots, 3 * quarter
    )
    compact = jnp.take(arrived, flat_from, axis=0).reshape(total_slots, 3, head_local, HD)
    heads_owner = patch_attention(compact, live_keys)
    bucket_from = jnp.clip(
        recv_off[:, None] + jnp.arange(bucket_rows, dtype=jnp.int32)[None, :], 0, total_slots - 1
    ).reshape(-1)
    going_home = jnp.take(heads_owner, bucket_from, axis=0).reshape(seg_count, bucket_rows, quarter)
    returned = lax.all_to_all(going_home, "seg", split_axis=0, concat_axis=0, tiled=True).reshape(
        total_slots, quarter
    )
    inverse = (
        jnp.zeros((rows_dev,), jnp.int32).at[send_order].set(jnp.arange(rows_dev, dtype=jnp.int32))
    )
    owner_of = jnp.minimum(
        jnp.sum((send_end[None, :] <= inverse[:, None]).astype(jnp.int32), axis=1), seg_count - 1
    )
    home_from = owner_of * bucket_rows + jnp.clip(inverse - send_off[owner_of], 0, bucket_rows - 1)
    heads_b = jnp.take(returned, home_from, axis=0)
    out_rows_two = lax.dynamic_slice_in_dim(out_second, ch_index * quarter, quarter, 0)
    partial_two = jnp.dot(heads_b, out_rows_two, preferred_element_type=jnp.float32)
    attn_two = lax.psum_scatter(
        partial_two.astype(jnp.bfloat16), "ch", scatter_dimension=1, tiled=True
    ).astype(jnp.float32)
    return (mixed_b_part.astype(jnp.float32) + attn_two).astype(jnp.bfloat16)


def solution(mesh):
    placed = (
        P("seg", None),
        P(None, "seg"),
        P("seg", None),
        P(),
        P(None, None, "ch"),
        P(None, None, "ch"),
        P(),
        P(None, None, "ch"),
        P(),
    )
    return jax.shard_map(
        local, mesh=mesh, in_specs=placed, out_specs=P("seg", "ch"), check_vma=False
    )
```

profile of v0, /device:TPU:8, one launch (start us, length us, event | category | flops | bytes accessed | tf_op | source)
XLA Modules:
  0.0 519.8 jit_solution(14209222011439790130)
XLA Ops:
  7.5 7.1 %collective-permute-start.1 = (bf16[128,256]{1,0:T(8,128)(2,1)S(1)}, bf16[128,256]{1,0:T(8,128)(2,1)S(1)}, u32[]{:S(2)}, u32[]{:S(2)}) collective-permute-start(bf16[128,256]{1,0:T(8,128)(2,1)S(1)} %get-tuple-element.486), channel_id=1, source_target_pairs={{4,0},{8,4},{12,8},{16,12},{20,16},{24,20},{28,24},{32,28},{36,32}... | collective-permute-start | bytes 196616 | tf_op jit(solution)/shard_map/ppermute | solution.py:24
  28.0 8.6 %gather_fusion.1 = s32[2048]{0:T(1024)S(1)} fusion(s32[1024]{0:T(1024)S(1)} %bitcast.276, s32[2048]{0:T(1024)S(1)} %broadcast_clamp_fusion.4), kind=kCustom, calls=%fused_computation.1 | custom fusion | bytes 24576 | tf_op jit(solution)/shard_map/gather | solution.py:132
  36.7 4.4 compare_select_fusion.9
  42.6 35.6 %select_select_fusion = s32[2048]{0:T(1024)S(1)} fusion(pred[2048]{0:T(1024)(128)(4,1)S(1)} %get-tuple-element.368, pred[2048]{0:T(1024)(128)(4,1)S(1)} %get-tuple-element.367, pred[2048]{0:T(1024)(128)(4,1)S(1)} %get-tuple-element.366, pred[2048]{0:T(1024)(128)(4,1)S(1)} %get-tuple-element.365, pred[2048]{0:T(1024)(128)(4,1)S(1)} %get-tuple-element.364, ...), kind=kLoop, calls=%fused_computation.244 | loop fusion | flops 116736 | bytes 133348 | tf_op jit(solution)/shard_map/gather | solution.py:140
  78.4 4.3 scatter_custom_fusion
  82.8 4.9 compare_select_fusion.18
  90.1 184.9 %while.55 = (s32[]{:T(128)}, f32[1024,64]{0,1:T(8,128)S(1)}, s32[27,1024]{1,0:T(8,128)}, s32[]{:T(128)}, bf16[1280,256]{1,0:T(8,128)(2,1)S(1)}, /*index=5*/bf16[27,256,64]{1,2,0:T(8,128)(2,1)}, s32[]{:T(128)}, s32[]{:T(128)}) while((s32[]{:T(128)}, f32[1024,64]{0,1:T(8,128)S(1)}, s32[27,1024]{1,0:T(8,128)}, s32[]{:T(128)}, ...), condition=%wide.region_1.2_spmd.clone, body=%wide.region_0.1_spmd.clone.sunk | while | flops 34223104 | bytes 2166903 | solution.py:116
  90.9 3.9 gather_fusion
  97.7 3.9 gather_fusion
  104.6 3.9 gather_fusion
  111.4 3.9 gather_fusion
  118.3 3.9 gather_fusion
  125.1 3.9 gather_fusion
  132.0 3.9 gather_fusion
  138.8 3.9 gather_fusion
  145.7 3.9 gather_fusion
  152.5 3.9 gather_fusion
  159.4 3.9 gather_fusion
  166.2 3.9 gather_fusion
  173.0 3.9 gather_fusion
  179.9 3.9 gather_fusion
  186.7 3.9 gather_fusion
  193.6 3.9 gather_fusion
  200.4 3.9 gather_fusion
  207.3 3.9 gather_fusion
  214.1 3.9 gather_fusion
  221.0 3.9 gather_fusion
  227.8 3.9 gather_fusion
  234.7 3.9 gather_fusion
  241.5 3.9 gather_fusion
  248.4 3.9 gather_fusion
  255.2 3.9 gather_fusion
  262.0 3.9 gather_fusion
  268.9 3.9 gather_fusion
  275.0 13.3 %all_gather.3 = bf16[1024,256]{0,1:T(8,128)(2,1)S(1)} all-gather(bf16[1024,64]{0,1:T(8,128)(2,1)S(1)} %add_convert_fusion.1), channel_id=1, replica_groups=mesh['seg'=64,'ch'=4] {'ch'}, dimensions={1}, use_global_device_ids=true | all-gather | bytes 655360 | tf_op jit(solution)/shard_map/all_gather | solution.py:119
  289.0 9.8 %while.52 = (s32[]{:T(128)}, bf16[2,512,4,16]{1,3,2,0:T(8,128)(2,1)S(1)}, bf16[2,512,4,16]{1,3,2,0:T(8,128)(2,1)S(1)}, bf16[1024,4,16]{0,2,1:T(8,128)(2,1)S(1)}, bf16[1024,4,16]{0,2,1:T(8,128)(2,1)S(1)}, /*index=5*/s32[]{:T(128)}) while((s32[]{:T(128)}, bf16[2,512,4,16]{1,3,2,0:T(8,128)(2,1)S(1)}, bf16[2,512,4,16]{1,3,2,0:T(8,128)(2,1)S(1)}, ...), condition=%wide.region_7.8_spmd, body=%wide.region_4.7_spmd.sunk | while | flops 151056384 | bytes 25600084 | solution.py:80
  301.0 45.8 %all-reduce.2.cloned.1.call-done = bf16[1024,256]{0,1:T(8,128)(2,1)} async-done(((bf16[1024,256]{0,1:T(8,128)(2,1)}), bf16[1024,256]{0,1:T(8,128)(2,1)}) %all-reduce.2.cloned.1.call-update) | async-done | bytes 524304 | tf_op jit(solution)/shard_map/psum | solution.py:124
  349.4 7.5 %gather_fusion.2 = bf16[2048,192]{1,0:T(8,128)(2,1)S(1)} fusion(bf16[1024,192]{1,0:T(8,128)(2,1)S(1)} %copy.62, s32[2048]{0:T(1024)S(1)} %broadcast_clamp_fusion.3), kind=kCustom, calls=%fused_computation.2 | custom fusion | bytes 1581056 | tf_op jit(solution)/shard_map/jit(_take)/gather | solution.py:145
  358.1 10.6 %all-to-all-start = ((bf16[64,32,192]{2,1,0:T(8,128)(2,1)}), bf16[64,32,192]{2,1,0:T(8,128)(2,1)S(1)}, u32[]{:S(2)}, u32[]{:S(2)}) async-start(bf16[64,32,192]{2,1,0:T(8,128)(2,1)} %broadcast_select_fusion.1), calls=%async_computation | async-start | bytes 2097152 | tf_op jit(solution)/shard_map/all_to_all | solution.py:148
  369.4 26.2 %all-to-all-done = bf16[64,32,192]{2,1,0:T(8,128)(2,1)S(1)} async-done(((bf16[64,32,192]{2,1,0:T(8,128)(2,1)}), bf16[64,32,192]{2,1,0:T(8,128)(2,1)S(1)}, u32[]{:S(2)}, u32[]{:S(2)}) %all-to-all-start) | async-done | bytes 786464 | tf_op jit(solution)/shard_map/all_to_all | solution.py:148
  395.6 7.5 %gather_fusion.3 = bf16[2048,192]{1,0:T(8,128)(2,1)S(1)} fusion(bf16[2048,192]{1,0:T(8,128)(2,1)S(1)} %bitcast.277, s32[2048]{0:T(1024)S(1)} %broadcast_clamp_fusion.2), kind=kCustom, calls=%fused_computation.3 | custom fusion | bytes 1581056 | tf_op jit(solution)/shard_map/jit(_take)/gather | solution.py:151
  405.5 22.2 %while.54 = (s32[]{:T(128)}, bf16[2,1024,64]{1,2,0:T(8,128)(2,1)S(1)}, bf16[2,1024,3,4,16]{1,4,3,2,0:T(8,128)(2,1)S(1)}, pred[2,1024]{1,0:T(4,128)(4,1)S(1)}, s32[]{:T(128)}, /*index=5*/s32[]{:T(128)}, s32[]{:T(128)}) while((s32[]{:T(128)}, bf16[2,1024,64]{1,2,0:T(8,128)(2,1)S(1)}, bf16[2,1024,3,4,16]{1,4,3,2,0:T(8,128)(2,1)S(1)}, ...), condition=%wide.region_22.23_spmd, body=%wide.region_17.22_spmd.sunk | while | flops 157347840 | bytes 28488956 | solution.py:82
  405.8 10.6 %while.56 = (s32[]{:T(128)}, bf16[2,512,4,16]{1,3,2,0:T(8,128)(2,1)S(1)}, pred[1024]{0:T(1024)(128)(4,1)S(1)}, bf16[2,512,4,16]{1,3,2,0:T(8,128)(2,1)S(1)}, bf16...) while((s32[]{:T(128)}, bf16[2,512,4,16]{1,3,2,0:T(8,128)(2,1)S(1)}, ...), condition=%wide.region_21.21_spmd, body=%wide.region_18.20_spmd.sunk | while | flops 157347840 | bytes 25603164 | solution.py:80
  416.9 10.6 %while.56 = (s32[]{:T(128)}, bf16[2,512,4,16]{1,3,2,0:T(8,128)(2,1)S(1)}, pred[1024]{0:T(1024)(128)(4,1)S(1)}, bf16[2,512,4,16]{1,3,2,0:T(8,128)(2,1)S(1)}, bf16...) while((s32[]{:T(128)}, bf16[2,512,4,16]{1,3,2,0:T(8,128)(2,1)S(1)}, ...), condition=%wide.region_21.21_spmd, body=%wide.region_18.20_spmd.sunk | while | flops 157347840 | bytes 25603164 | solution.py:80
  428.1 6.2 %gather_fusion.4 = bf16[2048,64]{1,0:T(8,128)(2,1)S(1)} fusion(bf16[2048,64]{1,0:T(8,128)(2,1)S(1)} %bitcast.278, s32[2048]{0:T(1024)S(1)} %copy-done.11), kind=kCustom, calls=%fused_computation.4 | custom fusion | bytes 532480 | tf_op jit(solution)/shard_map/jit(_take)/gather | solution.py:156
  435.6 7.8 %all-to-all-start.1 = ((bf16[64,2,1024]{2,1,0:T(2,128)(2,1)}), bf16[64,2,1024]{2,1,0:T(2,128)(2,1)S(1)}, u32[]{:S(2)}, u32[]{:S(2)}) async-start(bf16[64,2,1024]{2,1,0:T(2,128)(2,1)} %reshape.1017), calls=%async_computation.1 | async-start | bytes 524288 | tf_op jit(solution)/shard_map/all_to_all | solution.py:157
  444.6 36.5 %compare_and_fusion.4 = (pred[1024]{0:T(1024)(128)(4,1)S(1)}, s32[1024]{0:T(1024)S(1)}) fusion(s32[1024]{0:T(1024)S(1)} %copy-done.7, pred[1024]{0:T(1024)(128)(4,1)} %get-tuple-element.425, pred[1024]{0:T(1024)(128)(4,1)} %get-tuple-element.424, pred[1024]{0:T(1024)(128)(4,1)} %get-tuple-element.423, pred[1024]{0:T(1024)(128)(4,1)} %get-tuple-element.422, ...), kind=kLoop, calls=%fused_computation.258 | loop fusion | flops 69632 | bytes 76004 | tf_op jit(solution)/shard_map/jit(_take)/and | solution.py:167
  486.7 24.6 %reduce-scatter.4.cloned.1.call-done = bf16[64,1024]{1,0:T(8,128)(2,1)} async-done(((bf16[256,1024]{1,0:T(8,128)(2,1)}), bf16[64,1024]{1,0:T(8,128)(2,1)}) %reduce-scatter.4.cloned.1.call-update) | async-done | bytes 131088
  (358 shorter events, 146.3 us)
Async XLA Ops:
  6.5 292.5 %copy-start = (bf16[256,256]{1,0:T(8,128)(2,1)S(1)}, bf16[256,256]{1,0:T(8,128)(2,1)}, u32[]{:S(2)}) copy-start(bf16[256,256]{1,0:T(8,128)(2,1)} %param.23) | copy-start | bytes 393220
  6.5 340.2 %all-reduce.2.cloned.1.call-start = ((), (), s32[]{:S(2)}) async-start(), calls=%async_computation.3 | async-start | bytes 1048576 | tf_op jit(solution)/shard_map/psum | solution.py:124
  7.5 82.5 %collective-permute-start.1 = (bf16[128,256]{1,0:T(8,128)(2,1)S(1)}, bf16[128,256]{1,0:T(8,128)(2,1)S(1)}, u32[]{:S(2)}, u32[]{:S(2)}) collective-permute-start(bf16[128,256]{1,0:T(8,128)(2,1)S(1)} %get-tuple-element.486), channel_id=1, source_target_pairs={{4,0},{8,4},{12,8},{16,12},{20,16},{24,20},{28,24},{32,28},{36,32}... | collective-permute-start | bytes 196616 | tf_op jit(solution)/shard_map/ppermute | solution.py:24
  14.6 75.4 %collective-permute-start = (bf16[128,256]{1,0:T(8,128)(2,1)S(1)}, bf16[128,256]{1,0:T(8,128)(2,1)S(1)}, u32[]{:S(2)}, u32[]{:S(2)}) collective-permute-start(bf16[128,256]{1,0:T(8,128)(2,1)S(1)} %get-tuple-element.485), channel_id=1, source_target_pairs={{0,4},{4,8},{8,12},{12,16},{16,20},{20,24},{24,28},{28,32},{32,36}... | collective-permute-start | bytes 196616 | tf_op jit(solution)/shard_map/ppermute | solution.py:22
  24.5 64.7 %copy-start.3 = (s32[64]{0:T(128)}, s32[64]{0:T(128)S(1)}, u32[]{:S(2)}) copy-start(s32[64]{0:T(128)S(1)} %bitcast_subtract_fusion) | copy-start | bytes 772
  28.0 62.0 %copy-start.5 = (bf16[1024,256]{1,0:T(8,128)(2,1)S(1)}, bf16[1024,256]{1,0:T(8,128)(2,1)}, u32[]{:S(2)}) copy-start(bf16[1024,256]{1,0:T(8,128)(2,1)} %param.17) | copy-start | bytes 1572868
  90.0 198.5 %copy-start.47 = (bf16[256,3,64]{0,2,1:T(8,128)(2,1)S(1)}, bf16[256,3,64]{0,2,1:T(8,128)(2,1)}, u32[]{:S(2)}) copy-start(bf16[256,3,64]{0,2,1:T(8,128)(2,1)} %param.22) | copy-start | bytes 294916
  289.0 59.8 %copy-start.48 = (bf16[256,3,64]{0,2,1:T(8,128)(2,1)S(1)}, bf16[256,3,64]{0,2,1:T(8,128)(2,1)}, u32[]{:S(2)}) copy-start(bf16[256,3,64]{0,2,1:T(8,128)(2,1)} %param.24) | copy-start | bytes 294916
  358.1 37.5 %all-to-all-start = ((bf16[64,32,192]{2,1,0:T(8,128)(2,1)}), bf16[64,32,192]{2,1,0:T(8,128)(2,1)S(1)}, u32[]{:S(2)}, u32[]{:S(2)}) async-start(bf16[64,32,192]{2,1,0:T(8,128)(2,1)} %broadcast_select_fusion.1), calls=%async_computation | async-start | bytes 2097152 | tf_op jit(solution)/shard_map/all_to_all | solution.py:148
  405.2 39.0 %copy-start.7 = (s32[1024]{0:T(1024)S(1)}, s32[1024]{0:T(1024)}, u32[]{:S(2)}) copy-start(s32[1024]{0:T(1024)} %copy-done.6) | copy-start | bytes 12292
  405.2 39.0 %copy-start.9 = (s32[1024]{0:T(1024)S(1)}, s32[1024]{0:T(1024)}, u32[]{:S(2)}) copy-start(s32[1024]{0:T(1024)} %copy-done.8) | copy-start | bytes 12292
  405.2 39.0 %copy-start.12 = (s32[1024,1]{0,1:T(1,128)S(1)}, s32[1024,1]{0,1:T(1,128)}, u32[]{:S(2)}) copy-start(s32[1024,1]{0,1:T(1,128)} %get-tuple-element.472) | copy-start | bytes 12292
  405.2 39.0 %copy-start.13 = (pred[1024]{0:T(1024)(128)(4,1)S(1)}, pred[1024]{0:T(1024)(128)(4,1)}, u32[]{:S(2)}) copy-start(pred[1024]{0:T(1024)(128)(4,1)} %get-tuple-element.369) | copy-start | bytes 3076
  405.2 39.0 %copy-start.14 = (pred[1024]{0:T(1024)(128)(4,1)S(1)}, pred[1024]{0:T(1024)(128)(4,1)}, u32[]{:S(2)}) copy-start(pred[1024]{0:T(1024)(128)(4,1)} %get-tuple-element.370) | copy-start | bytes 3076
  405.2 39.0 %copy-start.15 = (pred[1024]{0:T(1024)(128)(4,1)S(1)}, pred[1024]{0:T(1024)(128)(4,1)}, u32[]{:S(2)}) copy-start(pred[1024]{0:T(1024)(128)(4,1)} %get-tuple-element.371) | copy-start | bytes 3076
  405.2 39.0 %copy-start.16 = (pred[1024]{0:T(1024)(128)(4,1)S(1)}, pred[1024]{0:T(1024)(128)(4,1)}, u32[]{:S(2)}) copy-start(pred[1024]{0:T(1024)(128)(4,1)} %get-tuple-element.372) | copy-start | bytes 3076
  405.2 39.0 %copy-start.17 = (pred[1024]{0:T(1024)(128)(4,1)S(1)}, pred[1024]{0:T(1024)(128)(4,1)}, u32[]{:S(2)}) copy-start(pred[1024]{0:T(1024)(128)(4,1)} %get-tuple-element.373) | copy-start | bytes 3076
  405.2 39.0 %copy-start.18 = (pred[1024]{0:T(1024)(128)(4,1)S(1)}, pred[1024]{0:T(1024)(128)(4,1)}, u32[]{:S(2)}) copy-start(pred[1024]{0:T(1024)(128)(4,1)} %get-tuple-element.374) | copy-start | bytes 3076
  405.2 39.0 %copy-start.19 = (pred[1024]{0:T(1024)(128)(4,1)S(1)}, pred[1024]{0:T(1024)(128)(4,1)}, u32[]{:S(2)}) copy-start(pred[1024]{0:T(1024)(128)(4,1)} %get-tuple-element.375) | copy-start | bytes 3076
  405.3 39.0 %copy-start.20 = (pred[1024]{0:T(1024)(128)(4,1)S(1)}, pred[1024]{0:T(1024)(128)(4,1)}, u32[]{:S(2)}) copy-start(pred[1024]{0:T(1024)(128)(4,1)} %get-tuple-element.376) | copy-start | bytes 3076
  405.3 39.0 %copy-start.21 = (pred[1024]{0:T(1024)(128)(4,1)S(1)}, pred[1024]{0:T(1024)(128)(4,1)}, u32[]{:S(2)}) copy-start(pred[1024]{0:T(1024)(128)(4,1)} %get-tuple-element.377) | copy-start | bytes 3076
  405.3 39.0 %copy-start.22 = (pred[1024]{0:T(1024)(128)(4,1)S(1)}, pred[1024]{0:T(1024)(128)(4,1)}, u32[]{:S(2)}) copy-start(pred[1024]{0:T(1024)(128)(4,1)} %get-tuple-element.378) | copy-start | bytes 3076
  405.3 39.0 %copy-start.23 = (pred[1024]{0:T(1024)(128)(4,1)S(1)}, pred[1024]{0:T(1024)(128)(4,1)}, u32[]{:S(2)}) copy-start(pred[1024]{0:T(1024)(128)(4,1)} %get-tuple-element.379) | copy-start | bytes 3076
  405.3 39.0 %copy-start.24 = (pred[1024]{0:T(1024)(128)(4,1)S(1)}, pred[1024]{0:T(1024)(128)(4,1)}, u32[]{:S(2)}) copy-start(pred[1024]{0:T(1024)(128)(4,1)} %get-tuple-element.380) | copy-start | bytes 3076
  405.3 39.0 %copy-start.25 = (pred[1024]{0:T(1024)(128)(4,1)S(1)}, pred[1024]{0:T(1024)(128)(4,1)}, u32[]{:S(2)}) copy-start(pred[1024]{0:T(1024)(128)(4,1)} %get-tuple-element.381) | copy-start | bytes 3076
  405.3 39.0 %copy-start.26 = (pred[1024]{0:T(1024)(128)(4,1)S(1)}, pred[1024]{0:T(1024)(128)(4,1)}, u32[]{:S(2)}) copy-start(pred[1024]{0:T(1024)(128)(4,1)} %get-tuple-element.382) | copy-start | bytes 3076
  405.3 39.0 %copy-start.27 = (pred[1024]{0:T(1024)(128)(4,1)S(1)}, pred[1024]{0:T(1024)(128)(4,1)}, u32[]{:S(2)}) copy-start(pred[1024]{0:T(1024)(128)(4,1)} %get-tuple-element.383) | copy-start | bytes 3076
  405.3 39.0 %copy-start.28 = (pred[1024]{0:T(1024)(128)(4,1)S(1)}, pred[1024]{0:T(1024)(128)(4,1)}, u32[]{:S(2)}) copy-start(pred[1024]{0:T(1024)(128)(4,1)} %get-tuple-element.384) | copy-start | bytes 3076
  405.3 39.0 %copy-start.29 = (pred[1024]{0:T(1024)(128)(4,1)S(1)}, pred[1024]{0:T(1024)(128)(4,1)}, u32[]{:S(2)}) copy-start(pred[1024]{0:T(1024)(128)(4,1)} %get-tuple-element.385) | copy-start | bytes 3076
  405.4 39.0 %copy-start.30 = (pred[1024]{0:T(1024)(128)(4,1)S(1)}, pred[1024]{0:T(1024)(128)(4,1)}, u32[]{:S(2)}) copy-start(pred[1024]{0:T(1024)(128)(4,1)} %get-tuple-element.386) | copy-start | bytes 3076
  405.4 39.0 %copy-start.31 = (pred[1024]{0:T(1024)(128)(4,1)S(1)}, pred[1024]{0:T(1024)(128)(4,1)}, u32[]{:S(2)}) copy-start(pred[1024]{0:T(1024)(128)(4,1)} %get-tuple-element.387) | copy-start | bytes 3076
  405.4 39.0 %copy-start.32 = (pred[1024]{0:T(1024)(128)(4,1)S(1)}, pred[1024]{0:T(1024)(128)(4,1)}, u32[]{:S(2)}) copy-start(pred[1024]{0:T(1024)(128)(4,1)} %get-tuple-element.388) | copy-start | bytes 3076
  405.4 39.0 %copy-start.33 = (pred[1024]{0:T(1024)(128)(4,1)S(1)}, pred[1024]{0:T(1024)(128)(4,1)}, u32[]{:S(2)}) copy-start(pred[1024]{0:T(1024)(128)(4,1)} %get-tuple-element.389) | copy-start | bytes 3076
  405.4 39.0 %copy-start.34 = (pred[1024]{0:T(1024)(128)(4,1)S(1)}, pred[1024]{0:T(1024)(128)(4,1)}, u32[]{:S(2)}) copy-start(pred[1024]{0:T(1024)(128)(4,1)} %get-tuple-element.390) | copy-start | bytes 3076
  405.4 39.0 %copy-start.35 = (pred[1024]{0:T(1024)(128)(4,1)S(1)}, pred[1024]{0:T(1024)(128)(4,1)}, u32[]{:S(2)}) copy-start(pred[1024]{0:T(1024)(128)(4,1)} %get-tuple-element.391) | copy-start | bytes 3076
  405.4 39.0 %copy-start.36 = (pred[1024]{0:T(1024)(128)(4,1)S(1)}, pred[1024]{0:T(1024)(128)(4,1)}, u32[]{:S(2)}) copy-start(pred[1024]{0:T(1024)(128)(4,1)} %get-tuple-element.392) | copy-start | bytes 3076
  405.4 39.0 %copy-start.37 = (pred[1024]{0:T(1024)(128)(4,1)S(1)}, pred[1024]{0:T(1024)(128)(4,1)}, u32[]{:S(2)}) copy-start(pred[1024]{0:T(1024)(128)(4,1)} %get-tuple-element.393) | copy-start | bytes 3076
  405.4 39.0 %copy-start.38 = (pred[1024]{0:T(1024)(128)(4,1)S(1)}, pred[1024]{0:T(1024)(128)(4,1)}, u32[]{:S(2)}) copy-start(pred[1024]{0:T(1024)(128)(4,1)} %get-tuple-element.394) | copy-start | bytes 3076
  405.4 39.0 %copy-start.39 = (pred[1024]{0:T(1024)(128)(4,1)S(1)}, pred[1024]{0:T(1024)(128)(4,1)}, u32[]{:S(2)}) copy-start(pred[1024]{0:T(1024)(128)(4,1)} %get-tuple-element.395) | copy-start | bytes 3076
  405.5 39.0 %copy-start.40 = (pred[1024]{0:T(1024)(128)(4,1)S(1)}, pred[1024]{0:T(1024)(128)(4,1)}, u32[]{:S(2)}) copy-start(pred[1024]{0:T(1024)(128)(4,1)} %get-tuple-element.396) | copy-start | bytes 3076
  405.5 39.0 %copy-start.41 = (pred[1024]{0:T(1024)(128)(4,1)S(1)}, pred[1024]{0:T(1024)(128)(4,1)}, u32[]{:S(2)}) copy-start(pred[1024]{0:T(1024)(128)(4,1)} %get-tuple-element.397) | copy-start | bytes 3076
  405.5 39.0 %copy-start.42 = (pred[1024]{0:T(1024)(128)(4,1)S(1)}, pred[1024]{0:T(1024)(128)(4,1)}, u32[]{:S(2)}) copy-start(pred[1024]{0:T(1024)(128)(4,1)} %get-tuple-element.398) | copy-start | bytes 3076
  405.5 39.0 %copy-start.43 = (pred[1024]{0:T(1024)(128)(4,1)S(1)}, pred[1024]{0:T(1024)(128)(4,1)}, u32[]{:S(2)}) copy-start(pred[1024]{0:T(1024)(128)(4,1)} %get-tuple-element.399) | copy-start | bytes 3076
  405.5 39.0 %copy-start.44 = (pred[1024]{0:T(1024)(128)(4,1)S(1)}, pred[1024]{0:T(1024)(128)(4,1)}, u32[]{:S(2)}) copy-start(pred[1024]{0:T(1024)(128)(4,1)} %get-tuple-element.400) | copy-start | bytes 3076
  405.5 39.0 %copy-start.45 = (pred[1024]{0:T(1024)(128)(4,1)S(1)}, pred[1024]{0:T(1024)(128)(4,1)}, u32[]{:S(2)}) copy-start(pred[1024]{0:T(1024)(128)(4,1)} %get-tuple-element.401) | copy-start | bytes 3076
  405.5 39.0 %copy-start.46 = (pred[1024]{0:T(1024)(128)(4,1)S(1)}, pred[1024]{0:T(1024)(128)(4,1)}, u32[]{:S(2)}) copy-start(pred[1024]{0:T(1024)(128)(4,1)} %get-tuple-element.402) | copy-start | bytes 3076
  435.6 45.5 %all-to-all-start.1 = ((bf16[64,2,1024]{2,1,0:T(2,128)(2,1)}), bf16[64,2,1024]{2,1,0:T(2,128)(2,1)S(1)}, u32[]{:S(2)}, u32[]{:S(2)}) async-start(bf16[64,2,1024]{2,1,0:T(2,128)(2,1)} %reshape.1017), calls=%async_computation.1 | async-start | bytes 524288 | tf_op jit(solution)/shard_map/all_to_all | solution.py:157
  443.4 67.9 %reduce-scatter.4.cloned.1.call-start = ((), (), s32[]{:S(2)}) async-start(), calls=%async_computation.4 | async-start | bytes 655360
  (7 other events, 127.1 us)
Sparse Core Ops, SparseCore 0:
  300.3 46.3 all-reduce.1
  486.8 24.4 reduce-scatter.3
where the time goes:
time: 527 us; the launch traced here: 520 us
  local copies, waits for them, and re-layouts  158 us (30%)
  other arithmetic  150 us (28%)
  waiting for transfers between devices  96.7 us (18%)
  matrix products  57.5 us (11%)
  starting transfers between devices  27.4 us (5%)
  between operations  14.6 us (3%)
  blocking collectives  13.3 us (3%)
    gather x27, local copies, waits for them, and re-layouts, conv_step(): picked = jnp.take(padded, local_row, axis=0)  106 us
    psum x1, waiting for transfers between devices, local(): lax.psum(partial_one.astype(jnp.bfloat16), 'ch').astype(jnp.float32)  45.8 us
    gather x3, other arithmetic, local(): within = jnp.clip(slots - recv_off[source], 0, bucket_rows - 1)  41.5 us
    and x1, other arithmetic, local(): heads_b = jnp.take(returned, home_from, axis=0)  36.5 us
    dot_general x27, matrix products, conv_step(): jnp.dot(picked, conv_weight[kernel_index], preferred_element_type=jnp.flo...  34.4 us
    all_to_all x1, waiting for transfers between devices, local(): lax.all_to_all(outgoing, 'seg', split_axis=0, concat_axis=0, tiled=True)  26.2 us
    unnamed x3, waiting for transfers between devices  24.6 us
    ge x27, other arithmetic, conv_step(): target >= 0  21.3 us
  transfers between devices with their start and end apart: 6, of which 3 were waited for; matrix products, arithmetic and copies ran while one was open for 22% of the time, Pallas kernels for 0%

commit v1 on v0

--- a/solution.py
+++ b/solution.py
@@ -121,7 +121,9 @@
     heads_a = patch_attention(qkv_a, jnp.ones((rows_dev,), bool))
     out_rows = lax.dynamic_slice_in_dim(out_first, ch_index * quarter, quarter, 0)
     partial_one = jnp.dot(heads_a, out_rows, preferred_element_type=jnp.float32)
-    attn_one = lax.psum(partial_one.astype(jnp.bfloat16), "ch").astype(jnp.float32)
+    attn_one = jnp.sum(lax.all_gather(partial_one.astype(jnp.bfloat16), "ch"), axis=0).astype(
+        jnp.float32
+    )
     mixed_b = (mixed_a.astype(jnp.float32) + attn_one).astype(jnp.bfloat16)
     mixed_b_part = lax.dynamic_slice_in_dim(mixed_b, ch_index * quarter, quarter, 1)
     counts_row = lax.dynamic_index_in_dim(send_counts, seg_index, 0, keepdims=False)

time: 527 us -> 481 us (0.913)
  waiting for transfers between devices: 96.7 us -> 51.1 us
    psum x1 -> x0, waiting for transfers between devices: 45.8 us -> none  [local(): lax.psum(partial_one.astype(jnp.bfloat16), 'ch').astype(jnp.float32)]
    reduce_scatter x0 -> x1, waiting for transfers between devices: none -> 24.8 us  [local(): lax.psum_scatter(partial_two.astype(jnp.bfloat16), 'ch', scatter_dimensio...]
    unnamed x3 -> x2, waiting for transfers between devices: 24.6 us -> 0.03 us
  transfers between devices with their start and end apart: 6 -> 6, of which waited for: 3 -> 2; matrix products, arithmetic and copies ran while one was open for 22% -> 24% of each run, Pallas kernels for 0% -> 0%
where the time goes in v1:
time: 481 us; the launch traced here: 474 us
  local copies, waits for them, and re-layouts  159 us (33%)
  other arithmetic  152 us (32%)
  matrix products  57.5 us (12%)
  waiting for transfers between devices  51.1 us (11%)
  starting transfers between devices  24.9 us (5%)
  between operations  14.6 us (3%)
  blocking collectives  13.1 us (3%)
    gather x27, local copies, waits for them, and re-layouts, conv_step(): picked = jnp.take(padded, local_row, axis=0)  106 us
    gather x3, other arithmetic, local(): within = jnp.clip(slots - recv_off[source], 0, bucket_rows - 1)  41.7 us
    and x1, other arithmetic, local(): heads_b = jnp.take(returned, home_from, axis=0)  36.5 us
    dot_general x27, matrix products, conv_step(): jnp.dot(picked, conv_weight[kernel_index], preferred_element_type=jnp.flo...  34.4 us
    all_to_all x1, waiting for transfers between devices, local(): lax.all_to_all(outgoing, 'seg', split_axis=0, concat_axis=0, tiled=True)  26.2 us
    reduce_scatter x1, waiting for transfers between devices, local(): lax.psum_scatter(partial_two.astype(jnp.bfloat16), 'ch', scatter_dimensio...  24.8 us
    ge x27, other arithmetic, conv_step(): target >= 0  21.3 us
    select_n x27, other arithmetic, conv_step(): picked = jnp.take(padded, local_row, axis=0)  21.1 us
  transfers between devices with their start and end apart: 6, of which 2 were waited for; matrix products, arithmetic and copies ran while one was open for 24% of the time, Pallas kernels for 0%

profile of v1, /device:TPU:8, one launch (start us, length us, event | category | flops | bytes accessed | tf_op | source)
XLA Modules:
  0.0 473.8 jit_solution(18340118177092279685)
XLA Ops:
  7.5 7.1 %collective-permute-start.1 = (bf16[128,256]{1,0:T(8,128)(2,1)S(1)}, bf16[128,256]{1,0:T(8,128)(2,1)S(1)}, u32[]{:S(2)}, u32[]{:S(2)}) collective-permute-start(bf16[128,256]{1,0:T(8,128)(2,1)S(1)} %get-tuple-element.471), channel_id=1, source_target_pairs={{4,0},{8,4},{12,8},{16,12},{20,16},{24,20},{28,24},{32,28},{36,32}... | collective-permute-start | bytes 196616 | tf_op jit(solution)/shard_map/ppermute | solution.py:24
  23.6 4.6 compare_select_fusion.9
  30.1 184.9 %while.55 = (s32[]{:T(128)}, f32[1024,64]{0,1:T(8,128)S(1)}, s32[27,1024]{1,0:T(8,128)}, s32[]{:T(128)}, bf16[1280,256]{1,0:T(8,128)(2,1)S(1)}, /*index=5*/bf16[27,256,64]{1,2,0:T(8,128)(2,1)}, s32[]{:T(128)}, s32[]{:T(128)}) while((s32[]{:T(128)}, f32[1024,64]{0,1:T(8,128)S(1)}, s32[27,1024]{1,0:T(8,128)}, s32[]{:T(128)}, ...), condition=%wide.region_1.2_spmd.clone, body=%wide.region_0.1_spmd.clone.sunk | while | flops 34223104 | bytes 2166903 | solution.py:116
  31.0 3.9 gather_fusion
  37.8 3.9 gather_fusion
  44.6 3.9 gather_fusion
  51.5 3.9 gather_fusion
  58.3 3.9 gather_fusion
  65.2 3.9 gather_fusion
  72.0 3.9 gather_fusion
  78.9 3.9 gather_fusion
  85.7 3.9 gather_fusion
  92.6 3.9 gather_fusion
  99.4 3.9 gather_fusion
  106.3 3.9 gather_fusion
  113.1 3.9 gather_fusion
  120.0 3.9 gather_fusion
  126.8 3.9 gather_fusion
  133.6 3.9 gather_fusion
  140.5 3.9 gather_fusion
  147.3 3.9 gather_fusion
  154.2 3.9 gather_fusion
  161.0 3.9 gather_fusion
  167.9 3.9 gather_fusion
  174.7 3.9 gather_fusion
  181.6 3.9 gather_fusion
  188.4 3.9 gather_fusion
  195.3 3.9 gather_fusion
  202.1 3.9 gather_fusion
  209.0 3.9 gather_fusion
  215.0 13.1 %all_gather.9 = bf16[1024,256]{0,1:T(8,128)(2,1)S(1)} all-gather(bf16[1024,64]{0,1:T(8,128)(2,1)S(1)} %add_convert_fusion.1), channel_id=1, replica_groups=mesh['seg'=64,'ch'=4] {'ch'}, dimensions={1}, use_global_device_ids=true | all-gather | bytes 655360 | tf_op jit(solution)/shard_map/all_gather | solution.py:119
  228.9 9.8 %while.52 = (s32[]{:T(128)}, bf16[2,512,4,16]{1,3,2,0:T(8,128)(2,1)S(1)}, bf16[2,512,4,16]{1,3,2,0:T(8,128)(2,1)S(1)}, bf16[1024,4,16]{0,2,1:T(8,128)(2,1)S(1)}, bf16[1024,4,16]{0,2,1:T(8,128)(2,1)S(1)}, /*index=5*/s32[]{:T(128)}) while((s32[]{:T(128)}, bf16[2,512,4,16]{1,3,2,0:T(8,128)(2,1)S(1)}, bf16[2,512,4,16]{1,3,2,0:T(8,128)(2,1)S(1)}, ...), condition=%wide.region_7.8_spmd, body=%wide.region_4.7_spmd.sunk | while | flops 151056384 | bytes 25600084 | solution.py:80
  240.8 8.6 %gather_fusion.1 = s32[2048]{0:T(1024)S(1)} fusion(s32[1024]{0:T(1024)S(1)} %bitcast.273, s32[2048]{0:T(1024)S(1)} %broadcast_clamp_fusion.4), kind=kCustom, calls=%fused_computation.1 | custom fusion | bytes 24576 | tf_op jit(solution)/shard_map/gather | solution.py:134
  250.9 35.6 %select_select_fusion = s32[2048]{0:T(1024)S(1)} fusion(pred[2048]{0:T(1024)(128)(4,1)S(1)} %get-tuple-element.353, pred[2048]{0:T(1024)(128)(4,1)S(1)} %get-tuple-element.352, pred[2048]{0:T(1024)(128)(4,1)S(1)} %get-tuple-element.351, pred[2048]{0:T(1024)(128)(4,1)S(1)} %get-tuple-element.350, pred[2048]{0:T(1024)(128)(4,1)S(1)} %get-tuple-element.349, ...), kind=kLoop, calls=%fused_computation.243 | loop fusion | flops 116736 | bytes 133348 | tf_op jit(solution)/shard_map/gather | solution.py:142
  286.8 4.5 scatter_custom_fusion
  294.2 5.2 %compare_select_fusion.18 = (s32[1024,1]{0,1:T(1,128)}, s32[1024,1]{0,1:T(1,128)S(1)}) fusion(s32[]{:T(128)} %bitcast.78, s32[]{:T(128)} %bitcast.79, s32[]{:T(128)} %bitcast.80, s32[]{:T(128)} %bitcast.81, s32[]{:T(128)} %bitcast.82, s32[]{:T(128)} %bitcast.84, s32[]{:T(128)} %bitcast.83, s32[1024,1]{0,1:T(1,128)S(1)} %bitcast.296), kind=kLoop, calls=%fused_computation.235 | loop fusion | flops 15360 | bytes 12316 | tf_op jit(solution)/shard_map/gather | solution.py:168
  305.6 7.5 %gather_fusion.2 = bf16[2048,192]{1,0:T(8,128)(2,1)S(1)} fusion(bf16[1024,192]{1,0:T(8,128)(2,1)S(1)} %copy.43, s32[2048]{0:T(1024)S(1)} %broadcast_clamp_fusion.3), kind=kCustom, calls=%fused_computation.2 | custom fusion | bytes 1581056 | tf_op jit(solution)/shard_map/jit(_take)/gather | solution.py:147
  314.4 8.0 %all-to-all-start = ((bf16[64,32,192]{2,1,0:T(8,128)(2,1)}), bf16[64,32,192]{2,1,0:T(8,128)(2,1)S(1)}, u32[]{:S(2)}, u32[]{:S(2)}) async-start(bf16[64,32,192]{2,1,0:T(8,128)(2,1)} %broadcast_select_fusion.1), calls=%async_computation | async-start | bytes 2097152 | tf_op jit(solution)/shard_map/all_to_all | solution.py:150
  323.1 26.2 %all-to-all-done = bf16[64,32,192]{2,1,0:T(8,128)(2,1)S(1)} async-done(((bf16[64,32,192]{2,1,0:T(8,128)(2,1)}), bf16[64,32,192]{2,1,0:T(8,128)(2,1)S(1)}, u32[]{:S(2)}, u32[]{:S(2)}) %all-to-all-start) | async-done | bytes 786464 | tf_op jit(solution)/shard_map/all_to_all | solution.py:150
  349.4 7.5 %gather_fusion.3 = bf16[2048,192]{1,0:T(8,128)(2,1)S(1)} fusion(bf16[2048,192]{1,0:T(8,128)(2,1)S(1)} %bitcast.274, s32[2048]{0:T(1024)S(1)} %broadcast_clamp_fusion.2), kind=kCustom, calls=%fused_computation.3 | custom fusion | bytes 1581056 | tf_op jit(solution)/shard_map/jit(_take)/gather | solution.py:153
  359.3 22.3 %while.54 = (s32[]{:T(128)}, bf16[2,1024,64]{1,2,0:T(8,128)(2,1)S(1)}, bf16[2,1024,3,4,16]{1,4,3,2,0:T(8,128)(2,1)S(1)}, pred[2,1024]{1,0:T(4,128)(4,1)S(1)}, s32[]{:T(128)}, /*index=5*/s32[]{:T(128)}, s32[]{:T(128)}) while((s32[]{:T(128)}, bf16[2,1024,64]{1,2,0:T(8,128)(2,1)S(1)}, bf16[2,1024,3,4,16]{1,4,3,2,0:T(8,128)(2,1)S(1)}, ...), condition=%wide.region_22.23_spmd, body=%wide.region_17.22_spmd.sunk | while | flops 157347840 | bytes 28488956 | solution.py:82
  359.5 10.7 %while.56 = (s32[]{:T(128)}, bf16[2,512,4,16]{1,3,2,0:T(8,128)(2,1)S(1)}, pred[1024]{0:T(1024)(128)(4,1)S(1)}, bf16[2,512,4,16]{1,3,2,0:T(8,128)(2,1)S(1)}, bf16...) while((s32[]{:T(128)}, bf16[2,512,4,16]{1,3,2,0:T(8,128)(2,1)S(1)}, ...), condition=%wide.region_21.21_spmd, body=%wide.region_18.20_spmd.sunk | while | flops 157347840 | bytes 25603164 | solution.py:80
  370.7 10.7 %while.56 = (s32[]{:T(128)}, bf16[2,512,4,16]{1,3,2,0:T(8,128)(2,1)S(1)}, pred[1024]{0:T(1024)(128)(4,1)S(1)}, bf16[2,512,4,16]{1,3,2,0:T(8,128)(2,1)S(1)}, bf16...) while((s32[]{:T(128)}, bf16[2,512,4,16]{1,3,2,0:T(8,128)(2,1)S(1)}, ...), condition=%wide.region_21.21_spmd, body=%wide.region_18.20_spmd.sunk | while | flops 157347840 | bytes 25603164 | solution.py:80
  381.9 6.2 %gather_fusion.4 = bf16[2048,64]{1,0:T(8,128)(2,1)S(1)} fusion(bf16[2048,64]{1,0:T(8,128)(2,1)S(1)} %bitcast.275, s32[2048]{0:T(1024)S(1)} %copy-done.10), kind=kCustom, calls=%fused_computation.4 | custom fusion | bytes 532480 | tf_op jit(solution)/shard_map/jit(_take)/gather | solution.py:158
  389.4 7.8 %all-to-all-start.1 = ((bf16[64,2,1024]{2,1,0:T(2,128)(2,1)}), bf16[64,2,1024]{2,1,0:T(2,128)(2,1)S(1)}, u32[]{:S(2)}, u32[]{:S(2)}) async-start(bf16[64,2,1024]{2,1,0:T(2,128)(2,1)} %reshape.1016), calls=%async_computation.1 | async-start | bytes 524288 | tf_op jit(solution)/shard_map/all_to_all | solution.py:159
  398.4 36.5 %compare_and_fusion.4 = (pred[1024]{0:T(1024)(128)(4,1)S(1)}, s32[1024]{0:T(1024)S(1)}) fusion(s32[1024]{0:T(1024)S(1)} %copy-done.6, pred[1024]{0:T(1024)(128)(4,1)} %get-tuple-element.410, pred[1024]{0:T(1024)(128)(4,1)} %get-tuple-element.409, pred[1024]{0:T(1024)(128)(4,1)} %get-tuple-element.408, pred[1024]{0:T(1024)(128)(4,1)} %get-tuple-element.407, ...), kind=kLoop, calls=%fused_computation.257 | loop fusion | flops 69632 | bytes 76004 | tf_op jit(solution)/shard_map/jit(_take)/and | solution.py:169
  435.3 3.2 gather_fusion.5
  440.5 24.8 %reduce-scatter.2.cloned.1.call-done = bf16[1024,64]{0,1:T(8,128)(2,1)} async-done(((bf16[1024,256]{0,1:T(8,128)(2,1)}), bf16[1024,64]{0,1:T(8,128)(2,1)}) %reduce-scatter.2.cloned.1.call-update) | async-done | bytes 131088 | tf_op jit(solution)/shard_map/reduce_scatter | solution.py:172
  (358 shorter events, 144.7 us)
Async XLA Ops:
  6.5 232.4 %copy-start = (bf16[256,256]{1,0:T(8,128)(2,1)S(1)}, bf16[256,256]{1,0:T(8,128)(2,1)}, u32[]{:S(2)}) copy-start(bf16[256,256]{1,0:T(8,128)(2,1)} %param.23) | copy-start | bytes 393220
  6.5 295.1 %all-gather.3.cloned.1.call-start = ((), (), s32[]{:S(2)}) async-start(), calls=%async_computation.4 | async-start | bytes 2621440 | tf_op jit(solution)/shard_map/all_gather | solution.py:124
  7.5 21.5 %collective-permute-start.1 = (bf16[128,256]{1,0:T(8,128)(2,1)S(1)}, bf16[128,256]{1,0:T(8,128)(2,1)S(1)}, u32[]{:S(2)}, u32[]{:S(2)}) collective-permute-start(bf16[128,256]{1,0:T(8,128)(2,1)S(1)} %get-tuple-element.471), channel_id=1, source_target_pairs={{4,0},{8,4},{12,8},{16,12},{20,16},{24,20},{28,24},{32,28},{36,32}... | collective-permute-start | bytes 196616 | tf_op jit(solution)/shard_map/ppermute | solution.py:24
  14.6 14.4 %collective-permute-start = (bf16[128,256]{1,0:T(8,128)(2,1)S(1)}, bf16[128,256]{1,0:T(8,128)(2,1)S(1)}, u32[]{:S(2)}, u32[]{:S(2)}) collective-permute-start(bf16[128,256]{1,0:T(8,128)(2,1)S(1)} %get-tuple-element.470), channel_id=1, source_target_pairs={{0,4},{4,8},{8,12},{12,16},{16,20},{20,24},{24,28},{28,32},{32,36}... | collective-permute-start | bytes 196616 | tf_op jit(solution)/shard_map/ppermute | solution.py:22
  23.4 269.9 %copy-start.3 = (s32[64]{0:T(128)}, s32[64]{0:T(128)S(1)}, u32[]{:S(2)}) copy-start(s32[64]{0:T(128)S(1)} %bitcast_subtract_fusion) | copy-start | bytes 772
  30.1 198.3 %copy-start.46 = (bf16[256,3,64]{0,2,1:T(8,128)(2,1)S(1)}, bf16[256,3,64]{0,2,1:T(8,128)(2,1)}, u32[]{:S(2)}) copy-start(bf16[256,3,64]{0,2,1:T(8,128)(2,1)} %param.22) | copy-start | bytes 294916
  240.8 64.3 %copy-start.47 = (bf16[256,3,64]{0,2,1:T(8,128)(2,1)S(1)}, bf16[256,3,64]{0,2,1:T(8,128)(2,1)}, u32[]{:S(2)}) copy-start(bf16[256,3,64]{0,2,1:T(8,128)(2,1)} %param.24) | copy-start | bytes 294916
  314.4 35.0 %all-to-all-start = ((bf16[64,32,192]{2,1,0:T(8,128)(2,1)}), bf16[64,32,192]{2,1,0:T(8,128)(2,1)S(1)}, u32[]{:S(2)}, u32[]{:S(2)}) async-start(bf16[64,32,192]{2,1,0:T(8,128)(2,1)} %broadcast_select_fusion.1), calls=%async_computation | async-start | bytes 2097152 | tf_op jit(solution)/shard_map/all_to_all | solution.py:150
  358.9 38.4 %copy-start.4 = (s32[64]{0:T(128)S(1)}, s32[64]{0:T(128)}, u32[]{:S(2)}) copy-start(s32[64]{0:T(128)} %copy-done.3) | copy-start | bytes 772
  358.9 39.1 %copy-start.6 = (s32[1024]{0:T(1024)S(1)}, s32[1024]{0:T(1024)}, u32[]{:S(2)}) copy-start(s32[1024]{0:T(1024)} %copy-done.5) | copy-start | bytes 12292
  358.9 39.1 %copy-start.8 = (s32[1024]{0:T(1024)S(1)}, s32[1024]{0:T(1024)}, u32[]{:S(2)}) copy-start(s32[1024]{0:T(1024)} %copy-done.7) | copy-start | bytes 12292
  358.9 39.1 %copy-start.11 = (s32[1024,1]{0,1:T(1,128)S(1)}, s32[1024,1]{0,1:T(1,128)}, u32[]{:S(2)}) copy-start(s32[1024,1]{0,1:T(1,128)} %get-tuple-element.457) | copy-start | bytes 12292
  358.9 39.1 %copy-start.12 = (pred[1024]{0:T(1024)(128)(4,1)S(1)}, pred[1024]{0:T(1024)(128)(4,1)}, u32[]{:S(2)}) copy-start(pred[1024]{0:T(1024)(128)(4,1)} %get-tuple-element.354) | copy-start | bytes 3076
  358.9 39.1 %copy-start.13 = (pred[1024]{0:T(1024)(128)(4,1)S(1)}, pred[1024]{0:T(1024)(128)(4,1)}, u32[]{:S(2)}) copy-start(pred[1024]{0:T(1024)(128)(4,1)} %get-tuple-element.355) | copy-start | bytes 3076
  359.0 39.1 %copy-start.14 = (pred[1024]{0:T(1024)(128)(4,1)S(1)}, pred[1024]{0:T(1024)(128)(4,1)}, u32[]{:S(2)}) copy-start(pred[1024]{0:T(1024)(128)(4,1)} %get-tuple-element.356) | copy-start | bytes 3076
  359.0 39.1 %copy-start.15 = (pred[1024]{0:T(1024)(128)(4,1)S(1)}, pred[1024]{0:T(1024)(128)(4,1)}, u32[]{:S(2)}) copy-start(pred[1024]{0:T(1024)(128)(4,1)} %get-tuple-element.357) | copy-start | bytes 3076
  359.0 39.1 %copy-start.16 = (pred[1024]{0:T(1024)(128)(4,1)S(1)}, pred[1024]{0:T(1024)(128)(4,1)}, u32[]{:S(2)}) copy-start(pred[1024]{0:T(1024)(128)(4,1)} %get-tuple-element.358) | copy-start | bytes 3076
  359.0 39.1 %copy-start.17 = (pred[1024]{0:T(1024)(128)(4,1)S(1)}, pred[1024]{0:T(1024)(128)(4,1)}, u32[]{:S(2)}) copy-start(pred[1024]{0:T(1024)(128)(4,1)} %get-tuple-element.359) | copy-start | bytes 3076
  359.0 39.1 %copy-start.18 = (pred[1024]{0:T(1024)(128)(4,1)S(1)}, pred[1024]{0:T(1024)(128)(4,1)}, u32[]{:S(2)}) copy-start(pred[1024]{0:T(1024)(128)(4,1)} %get-tuple-element.360) | copy-start | bytes 3076
  359.0 39.1 %copy-start.19 = (pred[1024]{0:T(1024)(128)(4,1)S(1)}, pred[1024]{0:T(1024)(128)(4,1)}, u32[]{:S(2)}) copy-start(pred[1024]{0:T(1024)(128)(4,1)} %get-tuple-element.361) | copy-start | bytes 3076
  359.0 39.1 %copy-start.20 = (pred[1024]{0:T(1024)(128)(4,1)S(1)}, pred[1024]{0:T(1024)(128)(4,1)}, u32[]{:S(2)}) copy-start(pred[1024]{0:T(1024)(128)(4,1)} %get-tuple-element.362) | copy-start | bytes 3076
  359.0 39.1 %copy-start.21 = (pred[1024]{0:T(1024)(128)(4,1)S(1)}, pred[1024]{0:T(1024)(128)(4,1)}, u32[]{:S(2)}) copy-start(pred[1024]{0:T(1024)(128)(4,1)} %get-tuple-element.363) | copy-start | bytes 3076
  359.0 39.1 %copy-start.22 = (pred[1024]{0:T(1024)(128)(4,1)S(1)}, pred[1024]{0:T(1024)(128)(4,1)}, u32[]{:S(2)}) copy-start(pred[1024]{0:T(1024)(128)(4,1)} %get-tuple-element.364) | copy-start | bytes 3076
  359.0 39.1 %copy-start.23 = (pred[1024]{0:T(1024)(128)(4,1)S(1)}, pred[1024]{0:T(1024)(128)(4,1)}, u32[]{:S(2)}) copy-start(pred[1024]{0:T(1024)(128)(4,1)} %get-tuple-element.365) | copy-start | bytes 3076
  359.1 39.1 %copy-start.24 = (pred[1024]{0:T(1024)(128)(4,1)S(1)}, pred[1024]{0:T(1024)(128)(4,1)}, u32[]{:S(2)}) copy-start(pred[1024]{0:T(1024)(128)(4,1)} %get-tuple-element.366) | copy-start | bytes 3076
  359.1 39.1 %copy-start.25 = (pred[1024]{0:T(1024)(128)(4,1)S(1)}, pred[1024]{0:T(1024)(128)(4,1)}, u32[]{:S(2)}) copy-start(pred[1024]{0:T(1024)(128)(4,1)} %get-tuple-element.367) | copy-start | bytes 3076
  359.1 39.1 %copy-start.26 = (pred[1024]{0:T(1024)(128)(4,1)S(1)}, pred[1024]{0:T(1024)(128)(4,1)}, u32[]{:S(2)}) copy-start(pred[1024]{0:T(1024)(128)(4,1)} %get-tuple-element.368) | copy-start | bytes 3076
  359.1 39.1 %copy-start.27 = (pred[1024]{0:T(1024)(128)(4,1)S(1)}, pred[1024]{0:T(1024)(128)(4,1)}, u32[]{:S(2)}) copy-start(pred[1024]{0:T(1024)(128)(4,1)} %get-tuple-element.369) | copy-start | bytes 3076
  359.1 39.1 %copy-start.28 = (pred[1024]{0:T(1024)(128)(4,1)S(1)}, pred[1024]{0:T(1024)(128)(4,1)}, u32[]{:S(2)}) copy-start(pred[1024]{0:T(1024)(128)(4,1)} %get-tuple-element.370) | copy-start | bytes 3076
  359.1 39.1 %copy-start.29 = (pred[1024]{0:T(1024)(128)(4,1)S(1)}, pred[1024]{0:T(1024)(128)(4,1)}, u32[]{:S(2)}) copy-start(pred[1024]{0:T(1024)(128)(4,1)} %get-tuple-element.371) | copy-start | bytes 3076
  359.1 39.1 %copy-start.30 = (pred[1024]{0:T(1024)(128)(4,1)S(1)}, pred[1024]{0:T(1024)(128)(4,1)}, u32[]{:S(2)}) copy-start(pred[1024]{0:T(1024)(128)(4,1)} %get-tuple-element.372) | copy-start | bytes 3076
  359.1 39.1 %copy-start.31 = (pred[1024]{0:T(1024)(128)(4,1)S(1)}, pred[1024]{0:T(1024)(128)(4,1)}, u32[]{:S(2)}) copy-start(pred[1024]{0:T(1024)(128)(4,1)} %get-tuple-element.373) | copy-start | bytes 3076
  359.1 39.1 %copy-start.32 = (pred[1024]{0:T(1024)(128)(4,1)S(1)}, pred[1024]{0:T(1024)(128)(4,1)}, u32[]{:S(2)}) copy-start(pred[1024]{0:T(1024)(128)(4,1)} %get-tuple-element.374) | copy-start | bytes 3076
  359.1 39.1 %copy-start.33 = (pred[1024]{0:T(1024)(128)(4,1)S(1)}, pred[1024]{0:T(1024)(128)(4,1)}, u32[]{:S(2)}) copy-start(pred[1024]{0:T(1024)(128)(4,1)} %get-tuple-element.375) | copy-start | bytes 3076
  359.2 39.1 %copy-start.34 = (pred[1024]{0:T(1024)(128)(4,1)S(1)}, pred[1024]{0:T(1024)(128)(4,1)}, u32[]{:S(2)}) copy-start(pred[1024]{0:T(1024)(128)(4,1)} %get-tuple-element.376) | copy-start | bytes 3076
  359.2 39.1 %copy-start.35 = (pred[1024]{0:T(1024)(128)(4,1)S(1)}, pred[1024]{0:T(1024)(128)(4,1)}, u32[]{:S(2)}) copy-start(pred[1024]{0:T(1024)(128)(4,1)} %get-tuple-element.377) | copy-start | bytes 3076
  359.2 39.1 %copy-start.36 = (pred[1024]{0:T(1024)(128)(4,1)S(1)}, pred[1024]{0:T(1024)(128)(4,1)}, u32[]{:S(2)}) copy-start(pred[1024]{0:T(1024)(128)(4,1)} %get-tuple-element.378) | copy-start | bytes 3076
  359.2 39.1 %copy-start.37 = (pred[1024]{0:T(1024)(128)(4,1)S(1)}, pred[1024]{0:T(1024)(128)(4,1)}, u32[]{:S(2)}) copy-start(pred[1024]{0:T(1024)(128)(4,1)} %get-tuple-element.379) | copy-start | bytes 3076
  359.2 39.1 %copy-start.38 = (pred[1024]{0:T(1024)(128)(4,1)S(1)}, pred[1024]{0:T(1024)(128)(4,1)}, u32[]{:S(2)}) copy-start(pred[1024]{0:T(1024)(128)(4,1)} %get-tuple-element.380) | copy-start | bytes 3076
  359.2 39.1 %copy-start.39 = (pred[1024]{0:T(1024)(128)(4,1)S(1)}, pred[1024]{0:T(1024)(128)(4,1)}, u32[]{:S(2)}) copy-start(pred[1024]{0:T(1024)(128)(4,1)} %get-tuple-element.381) | copy-start | bytes 3076
  359.2 39.1 %copy-start.40 = (pred[1024]{0:T(1024)(128)(4,1)S(1)}, pred[1024]{0:T(1024)(128)(4,1)}, u32[]{:S(2)}) copy-start(pred[1024]{0:T(1024)(128)(4,1)} %get-tuple-element.382) | copy-start | bytes 3076
  359.2 39.1 %copy-start.41 = (pred[1024]{0:T(1024)(128)(4,1)S(1)}, pred[1024]{0:T(1024)(128)(4,1)}, u32[]{:S(2)}) copy-start(pred[1024]{0:T(1024)(128)(4,1)} %get-tuple-element.383) | copy-start | bytes 3076
  359.2 39.1 %copy-start.42 = (pred[1024]{0:T(1024)(128)(4,1)S(1)}, pred[1024]{0:T(1024)(128)(4,1)}, u32[]{:S(2)}) copy-start(pred[1024]{0:T(1024)(128)(4,1)} %get-tuple-element.384) | copy-start | bytes 3076
  359.2 39.1 %copy-start.43 = (pred[1024]{0:T(1024)(128)(4,1)S(1)}, pred[1024]{0:T(1024)(128)(4,1)}, u32[]{:S(2)}) copy-start(pred[1024]{0:T(1024)(128)(4,1)} %get-tuple-element.385) | copy-start | bytes 3076
  359.3 39.1 %copy-start.44 = (pred[1024]{0:T(1024)(128)(4,1)S(1)}, pred[1024]{0:T(1024)(128)(4,1)}, u32[]{:S(2)}) copy-start(pred[1024]{0:T(1024)(128)(4,1)} %get-tuple-element.386) | copy-start | bytes 3076
  359.3 39.1 %copy-start.45 = (pred[1024]{0:T(1024)(128)(4,1)S(1)}, pred[1024]{0:T(1024)(128)(4,1)}, u32[]{:S(2)}) copy-start(pred[1024]{0:T(1024)(128)(4,1)} %get-tuple-element.387) | copy-start | bytes 3076
  389.4 45.5 %all-to-all-start.1 = ((bf16[64,2,1024]{2,1,0:T(2,128)(2,1)}), bf16[64,2,1024]{2,1,0:T(2,128)(2,1)S(1)}, u32[]{:S(2)}, u32[]{:S(2)}) async-start(bf16[64,2,1024]{2,1,0:T(2,128)(2,1)} %reshape.1016), calls=%async_computation.1 | async-start | bytes 524288 | tf_op jit(solution)/shard_map/all_to_all | solution.py:159
  397.2 68.1 %reduce-scatter.2.cloned.1.call-start = ((), (), s32[]{:S(2)}) async-start(), calls=%async_computation.3 | async-start | bytes 655360 | tf_op jit(solution)/shard_map/reduce_scatter | solution.py:172
  (6 other events, 87.2 us)
Sparse Core Ops, SparseCore 0:
  240.2 31.4 all-gather.2
  440.7 24.6 reduce-scatter.1
